TPU v7x, 32 devices: a whole 2x2x4 slice. The times are simulated.
32 devices in a mesh: rep: 8 (over y, x, core), fsdp: 4 (over z).
Axes of the slice: x: 2, y: 2, z: 4, core: 2. Of those that a mesh axis runs over, the one named last changes fastest.
Arguments:
- tokens: bfloat16 [8192, 1024], P(('rep', 'fsdp')), may hold values from -6 to 6
- doc_lengths: int32 [32, 8], P(('rep', 'fsdp')), may hold values from 0 to 256, as said below
- attn_norm: bfloat16 [1024], P('fsdp'), may hold values from 0.5 to 1.5
- w_query: bfloat16 [1024, 2048], P('fsdp'), may hold values from -0.1875 to 0.1875
- key_matrix: bfloat16 [1024, 1024], P('fsdp'), may hold values from -0.1875 to 0.1875
- value_matrix: bfloat16 [1024, 1024], P('fsdp'), may hold values from -0.1875 to 0.1875
- head_norms: bfloat16 [2, 128], replicated, may hold values from 0.25 to 1.75
- w_out: bfloat16 [2048, 1024], P('fsdp'), may hold values from -0.5 to 0.5
- ffn_norm: bfloat16 [1024], P('fsdp'), may hold values from 0.5 to 1.5
- w_gate: bfloat16 [1024, 3072], P('fsdp'), may hold values from -0.1875 to 0.1875
- w_up: bfloat16 [1024, 3072], P('fsdp'), may hold values from -0.1875 to 0.1875
- w_down: bfloat16 [3072, 1024], P('fsdp'), may hold values from -0.109375 to 0.109375
- cotangent: bfloat16 [8192, 1024], P(('rep', 'fsdp')), may hold values from -6 to 6
Outputs:
- mixed: bfloat16 [8192, 1024], P(('rep', 'fsdp'))
- d_tokens: bfloat16 [8192, 1024], P(('rep', 'fsdp'))
- d_attn_norm: float32 [1024], P('fsdp')
- d_w_query: float32 [1024, 2048], P('fsdp')
- d_w_key: float32 [1024, 1024], P('fsdp')
- d_w_value: float32 [1024, 1024], P('fsdp')
- d_head_norms: float32 [2, 128], replicated
- d_w_out: float32 [2048, 1024], P('fsdp')
- d_ffn_norm: float32 [1024], P('fsdp')
- d_w_gate: float32 [1024, 3072], P('fsdp')
- d_w_up: float32 [1024, 3072], P('fsdp')
- d_w_down: float32 [3072, 1024], P('fsdp')
Inputs may be any that keep to these rules, and one draw needn't show every extreme that they name: `doc_lengths`: row j lists the sequences packed from the first token row of device block j onward; zeros are empty slots; each row sums to 128 or more and to 256 or less; in every draw some device holds one sequence of 256 tokens.
All inputs are finite; a program needn't handle non-finite values.
Results may differ from a plain program's by a relative error of at most 0.02.
Values may be sent and summed in bfloat16 or wider, within the bound.
A program may use at most 192 MiB of HBM per device.

v0:
```python
import math
import jax
import jax.numpy as jnp
from jax import lax
from jax.sharding import PartitionSpec as P

QUERY_HEADS = 16
KEY_VALUE_HEADS = 8
HEAD_WIDTH = 128
EPS = 1e-06
ROPE_BASE = 1000000.0
NEG_FILL = -1e30


def layout(lengths, count_of_rows):
    seq_ends = jnp.cumsum(lengths)
    seq_starts = seq_ends - lengths
    row_ids = jnp.arange(count_of_rows, dtype=jnp.int32)
    segment = jnp.sum((row_ids[:, None] >= seq_ends[None, :]).astype(jnp.int32), axis=1)
    slot_ids = jnp.arange(lengths.shape[0], dtype=jnp.int32)
    member = (segment[:, None] == slot_ids[None, :]).astype(jnp.int32)
    position = row_ids - jnp.sum(member * seq_starts[None, :], axis=1)
    live_rows = row_ids < seq_ends[-1]
    causal = (
        (segment[:, None] == segment[None, :])
        & (row_ids[None, :] <= row_ids[:, None])
        & live_rows[:, None]
    )
    allowed = causal | (row_ids[:, None] == row_ids[None, :])
    return (position, live_rows, allowed)


def rope_tables(position, width):
    half_width = width // 2
    index = jnp.arange(half_width, dtype=jnp.float32)
    freq_table = jnp.exp(index * (-2.0 * math.log(ROPE_BASE) / width))
    angle = position.astype(jnp.float32)[:, None] * freq_table[None, :]
    return (jnp.cos(angle), jnp.sin(angle))


def apply_rotation(values_in, cosine_table, sine_table):
    half_width = values_in.shape[-1] // 2
    first_half = values_in[..., :half_width]
    second_half = values_in[..., half_width:]
    cos_rows = cosine_table[:, None, :]
    sin_rows = sine_table[:, None, :]
    return jnp.concatenate(
        [
            first_half * cos_rows - second_half * sin_rows,
            second_half * cos_rows + first_half * sin_rows,
        ],
        axis=-1,
    )


def rows_product(left, right):
    return lax.dot_general(
        left, right, (((0,), (0,)), ((), ())), preferred_element_type=jnp.float32
    )


def cols_product(left, right):
    return lax.dot_general(
        left, right, (((1,), (1,)), ((), ())), preferred_element_type=jnp.float32
    )


def norm_back(grad_in, hat_rows, row_scale, gain_full):
    leading_axes = tuple(range(grad_in.ndim - 1))
    grad_gain = jnp.sum(grad_in * hat_rows, axis=leading_axes)
    scaled_grad = grad_in * gain_full
    centered = scaled_grad - hat_rows * jnp.mean(scaled_grad * hat_rows, axis=-1, keepdims=True)
    return (row_scale * centered, grad_gain)


def head_stats(values_in):
    head_scale = lax.rsqrt(jnp.mean(values_in * values_in, axis=2, keepdims=True) + EPS)
    return (values_in * head_scale, head_scale)


def per_device(
    tokens,
    doc_lengths,
    attn_norm,
    w_query,
    key_matrix,
    value_matrix,
    head_norms,
    w_out,
    ffn_norm,
    w_gate,
    w_up,
    w_down,
    cotangent,
):
    count_of_rows = tokens.shape[0]
    group_width = QUERY_HEADS // KEY_VALUE_HEADS
    score_scale = HEAD_WIDTH ** (-0.5)
    fsdp_count = lax.axis_size("fsdp")
    rep_count = lax.axis_size("rep")
    position, live_rows, allowed = layout(doc_lengths[0], count_of_rows)
    cosine_table, sine_table = rope_tables(position, HEAD_WIDTH)
    head_gains = head_norms.astype(jnp.float32)
    query_full, key_full, value_full, out_full, norm_one = (
        lax.all_gather(w_query, "fsdp", axis=0, tiled=True),
        lax.all_gather(key_matrix, "fsdp", axis=0, tiled=True),
        lax.all_gather(value_matrix, "fsdp", axis=0, tiled=True),
        lax.all_gather(w_out, "fsdp", axis=0, tiled=True),
        lax.all_gather(attn_norm, "fsdp", axis=0, tiled=True),
    )
    inputs = tokens.astype(jnp.float32)
    first_scale = lax.rsqrt(jnp.mean(inputs * inputs, axis=1, keepdims=True) + EPS)
    first_hat = inputs * first_scale
    normalized_rows = (first_hat * norm_one).astype(jnp.bfloat16)
    query = jnp.dot(normalized_rows, query_full, preferred_element_type=jnp.float32).reshape(
        count_of_rows, QUERY_HEADS, HEAD_WIDTH
    )
    keys_before_rotation = jnp.dot(
        normalized_rows, key_full, preferred_element_type=jnp.float32
    ).reshape(count_of_rows, KEY_VALUE_HEADS, HEAD_WIDTH)
    value_rows = jnp.dot(normalized_rows, value_full, preferred_element_type=jnp.float32).astype(
        jnp.bfloat16
    )
    query_hat, query_scale = head_stats(query)
    key_hat, key_scale = head_stats(keys_before_rotation)
    rotated_query = apply_rotation(query_hat * head_gains[0], cosine_table, sine_table).astype(
        jnp.bfloat16
    )
    key_rot = apply_rotation(key_hat * head_gains[1], cosine_table, sine_table).astype(jnp.bfloat16)
    query_head_rows = jnp.moveaxis(
        rotated_query.reshape(count_of_rows, KEY_VALUE_HEADS, group_width, HEAD_WIDTH), 1, 0
    )
    key_heads = jnp.moveaxis(key_rot, 1, 0)
    value_head_rows = jnp.moveaxis(
        value_rows.reshape(count_of_rows, KEY_VALUE_HEADS, HEAD_WIDTH), 1, 0
    )

    def masked_scores(query_j, key_j):
        scores = (
            jnp.einsum("tgd,sd->gts", query_j, key_j, preferred_element_type=jnp.float32)
            * score_scale
        )
        return jnp.where(allowed[None], scores, NEG_FILL)

    def attend(parts):
        query_j, key_j, value_j = parts
        scores = masked_scores(query_j, key_j)
        highest = jnp.max(scores, axis=2, keepdims=True)
        expd = jnp.exp(scores - highest)
        totals = jnp.sum(expd, axis=2, keepdims=True)
        probs = (expd / totals).astype(jnp.bfloat16)
        head_out = jnp.einsum("gts,sd->tgd", probs, value_j, preferred_element_type=jnp.float32)
        return (head_out.astype(jnp.bfloat16), (highest + jnp.log(totals))[..., 0])

    mixed_heads, lse_heads = lax.map(attend, (query_head_rows, key_heads, value_head_rows))
    attended = jnp.moveaxis(mixed_heads, 0, 1).reshape(count_of_rows, QUERY_HEADS * HEAD_WIDTH)
    hidden = inputs + jnp.dot(attended, out_full, preferred_element_type=jnp.float32)
    gate_full, up_full, down_full, norm_two = (
        lax.all_gather(w_gate, "fsdp", axis=0, tiled=True),
        lax.all_gather(w_up, "fsdp", axis=0, tiled=True),
        lax.all_gather(w_down, "fsdp", axis=0, tiled=True),
        lax.all_gather(ffn_norm, "fsdp", axis=0, tiled=True),
    )
    second_scale = lax.rsqrt(jnp.mean(hidden * hidden, axis=1, keepdims=True) + EPS)
    second_hat = hidden * second_scale
    normed_two = (second_hat * norm_two).astype(jnp.bfloat16)
    gate = jnp.dot(normed_two, gate_full, preferred_element_type=jnp.float32)
    up_part = jnp.dot(normed_two, up_full, preferred_element_type=jnp.float32)
    sigma = jax.nn.sigmoid(gate)
    activated = (gate * sigma * up_part).astype(jnp.bfloat16)
    output = hidden + jnp.dot(activated, down_full, preferred_element_type=jnp.float32)
    mixed = jnp.where(live_rows[:, None], output, 0.0).astype(jnp.bfloat16)
    gate_full, up_full, down_full, norm_two = (
        lax.all_gather(w_gate, "fsdp", axis=0, tiled=True),
        lax.all_gather(w_up, "fsdp", axis=0, tiled=True),
        lax.all_gather(w_down, "fsdp", axis=0, tiled=True),
        lax.all_gather(ffn_norm, "fsdp", axis=0, tiled=True),
    )
    d_output = jnp.where(live_rows[:, None], cotangent.astype(jnp.float32), 0.0)
    d_branch = d_output.astype(jnp.bfloat16)
    grad_down = rows_product(activated, d_branch)
    d_activated = cols_product(d_branch, down_full)
    d_gate = (d_activated * up_part * sigma * (1.0 + gate * (1.0 - sigma))).astype(jnp.bfloat16)
    d_up = (d_activated * gate * sigma).astype(jnp.bfloat16)
    grad_gate = rows_product(normed_two, d_gate)
    grad_up = rows_product(normed_two, d_up)
    d_normed_two = cols_product(d_gate, gate_full) + cols_product(d_up, up_full)
    d_hidden_norm, grad_norm_two = norm_back(d_normed_two, second_hat, second_scale, norm_two)
    d_hidden = d_output + d_hidden_norm
    ffn_shards = (
        lax.psum_scatter(
            grad_gate.astype(jnp.bfloat16), "fsdp", scatter_dimension=0, tiled=True
        ).astype(jnp.float32),
        lax.psum_scatter(
            grad_up.astype(jnp.bfloat16), "fsdp", scatter_dimension=0, tiled=True
        ).astype(jnp.float32),
        lax.psum_scatter(
            grad_down.astype(jnp.bfloat16), "fsdp", scatter_dimension=0, tiled=True
        ).astype(jnp.float32),
        lax.psum_scatter(
            grad_norm_two.astype(jnp.bfloat16), "fsdp", scatter_dimension=0, tiled=True
        ).astype(jnp.float32),
    )
    ffn_sums = (
        lax.psum(ffn_shards[0].astype(jnp.bfloat16), "rep").astype(jnp.float32),
        lax.psum(ffn_shards[1].astype(jnp.bfloat16), "rep").astype(jnp.float32),
        lax.psum(ffn_shards[2].astype(jnp.bfloat16), "rep").astype(jnp.float32),
        lax.psum(ffn_shards[3].astype(jnp.bfloat16), "rep").astype(jnp.float32),
    )
    query_full, key_full, value_full, out_full, norm_one = (
        lax.all_gather(w_query, "fsdp", axis=0, tiled=True),
        lax.all_gather(key_matrix, "fsdp", axis=0, tiled=True),
        lax.all_gather(value_matrix, "fsdp", axis=0, tiled=True),
        lax.all_gather(w_out, "fsdp", axis=0, tiled=True),
        lax.all_gather(attn_norm, "fsdp", axis=0, tiled=True),
    )
    d_attn = d_hidden.astype(jnp.bfloat16)
    grad_out = rows_product(attended, d_attn)
    attended_gradient = cols_product(d_attn, out_full).astype(jnp.bfloat16)
    head_gradients = jnp.moveaxis(
        attended_gradient.reshape(count_of_rows, KEY_VALUE_HEADS, group_width, HEAD_WIDTH), 1, 0
    )

    def attend_back(parts):
        query_j, key_j, value_j, grad_j, lse_j = parts
        scores = masked_scores(query_j, key_j)
        probs = jnp.exp(scores - lse_j[..., None])
        d_probs = jnp.einsum("tgd,sd->gts", grad_j, value_j, preferred_element_type=jnp.float32)
        center = jnp.sum(probs * d_probs, axis=2, keepdims=True)
        d_scores = (probs * (d_probs - center)).astype(jnp.bfloat16)
        d_value_j = jnp.einsum(
            "gts,tgd->sd", probs.astype(jnp.bfloat16), grad_j, preferred_element_type=jnp.float32
        )
        d_query_j = (
            jnp.einsum("gts,sd->tgd", d_scores, key_j, preferred_element_type=jnp.float32)
            * score_scale
        )
        d_key_j = (
            jnp.einsum("gts,tgd->sd", d_scores, query_j, preferred_element_type=jnp.float32)
            * score_scale
        )
        return (d_query_j, d_key_j, d_value_j)

    d_query_heads, d_key_heads, value_head_gradient = lax.map(
        attend_back, (query_head_rows, key_heads, value_head_rows, head_gradients, lse_heads)
    )
    d_query_rot = jnp.moveaxis(d_query_heads, 0, 1).reshape(count_of_rows, QUERY_HEADS, HEAD_WIDTH)
    rotated_key_gradient = jnp.moveaxis(d_key_heads, 0, 1)
    query_norm_grad = apply_rotation(d_query_rot, cosine_table, -sine_table)
    key_norm_grad = apply_rotation(rotated_key_gradient, cosine_table, -sine_table)
    query_pre_grad, grad_query_gain = norm_back(
        query_norm_grad, query_hat, query_scale, head_gains[0]
    )
    key_pre_grad, grad_key_gain = norm_back(key_norm_grad, key_hat, key_scale, head_gains[1])
    d_query = query_pre_grad.reshape(count_of_rows, QUERY_HEADS * HEAD_WIDTH).astype(jnp.bfloat16)
    key_gradient = key_pre_grad.reshape(count_of_rows, KEY_VALUE_HEADS * HEAD_WIDTH).astype(
        jnp.bfloat16
    )
    value_gradient = (
        jnp.moveaxis(value_head_gradient, 0, 1)
        .reshape(count_of_rows, KEY_VALUE_HEADS * HEAD_WIDTH)
        .astype(jnp.bfloat16)
    )
    head_norm_sums = lax.psum(jnp.stack([grad_query_gain, grad_key_gain]), ("rep", "fsdp"))
    grad_query = rows_product(normalized_rows, d_query)
    grad_key = rows_product(normalized_rows, key_gradient)
    grad_value = rows_product(normalized_rows, value_gradient)
    d_normed = (
        cols_product(d_query, query_full)
        + cols_product(key_gradient, key_full)
        + cols_product(value_gradient, value_full)
    )
    d_input_norm, grad_norm_one = norm_back(d_normed, first_hat, first_scale, norm_one)
    d_tokens = (d_hidden + d_input_norm).astype(jnp.bfloat16)
    attn_shards = (
        lax.psum_scatter(
            grad_query.astype(jnp.bfloat16), "fsdp", scatter_dimension=0, tiled=True
        ).astype(jnp.float32),
        lax.psum_scatter(
            grad_key.astype(jnp.bfloat16), "fsdp", scatter_dimension=0, tiled=True
        ).astype(jnp.float32),
        lax.psum_scatter(
            grad_value.astype(jnp.bfloat16), "fsdp", scatter_dimension=0, tiled=True
        ).astype(jnp.float32),
        lax.psum_scatter(
            grad_out.astype(jnp.bfloat16), "fsdp", scatter_dimension=0, tiled=True
        ).astype(jnp.float32),
        lax.psum_scatter(
            grad_norm_one.astype(jnp.bfloat16), "fsdp", scatter_dimension=0, tiled=True
        ).astype(jnp.float32),
    )
    attn_sums = (
        lax.psum(attn_shards[0].astype(jnp.bfloat16), "rep").astype(jnp.float32),
        lax.psum(attn_shards[1].astype(jnp.bfloat16), "rep").astype(jnp.float32),
        lax.psum(attn_shards[2].astype(jnp.bfloat16), "rep").astype(jnp.float32),
        lax.psum(attn_shards[3].astype(jnp.bfloat16), "rep").astype(jnp.float32),
        lax.psum(attn_shards[4].astype(jnp.bfloat16), "rep").astype(jnp.float32),
    )
    grad_scale = 1.0 / math.sqrt(count_of_rows * rep_count * fsdp_count)
    return (
        mixed,
        d_tokens,
        attn_sums[4] * grad_scale,
        attn_sums[0] * grad_scale,
        attn_sums[1] * grad_scale,
        attn_sums[2] * grad_scale,
        head_norm_sums * grad_scale,
        attn_sums[3] * grad_scale,
        ffn_sums[3] * grad_scale,
        ffn_sums[0] * grad_scale,
        ffn_sums[1] * grad_scale,
        ffn_sums[2] * grad_scale,
    )


def solution(mesh):
    return jax.shard_map(
        per_device,
        mesh=mesh,
        in_specs=(
            P(("rep", "fsdp"), None),
            P(("rep", "fsdp"), None),
            P("fsdp"),
            P("fsdp", None),
            P("fsdp", None),
            P("fsdp", None),
            P(),
            P("fsdp", None),
            P("fsdp"),
            P("fsdp", None),
            P("fsdp", None),
            P("fsdp", None),
            P(("rep", "fsdp"), None),
        ),
        out_specs=(
            P(("rep", "fsdp"), None),
            P(("rep", "fsdp"), None),
            P("fsdp"),
            P("fsdp", None),
            P("fsdp", None),
            P("fsdp", None),
            P(),
            P("fsdp", None),
            P("fsdp"),
            P("fsdp", None),
            P("fsdp", None),
            P("fsdp", None),
        ),
        check_vma=False,
    )
```

profile of v0, /device:TPU:0, one launch (start us, length us, event | category | flops | bytes accessed | tf_op | source)
XLA Modules:
  0.0 1459.2 jit_solution(5098814045108164669)
XLA Ops:
  12.8 12.7 all-gather
  27.7 7.8 all-gather.1
  37.2 21.1 %all-gather.12.cloned.1.call-done = bf16[1024,1024]{1,0:T(8,128)(2,1)} async-done(((bf16[256,1024]{1,0:T(8,128)(2,1)}), bf16[1024,1024]{1,0:T(8,128)(2,1)}) %all-gather.12.cloned.1.call-update) | async-done | bytes 2097168 | tf_op jit(solution)/shard_map/all_gather | solution.py:106
  62.4 42.1 %all-gather.10.cloned.1.call-done = bf16[1024,1024]{1,0:T(8,128)(2,1)} async-done(((bf16[256,1024]{1,0:T(8,128)(2,1)}), bf16[1024,1024]{1,0:T(8,128)(2,1)}) %all-gather.10.cloned.1.call-update) | async-done | bytes 2097168 | tf_op jit(solution)/shard_map/all_gather | solution.py:107
  109.8 75.8 %all-gather.14.cloned.1.call-done = bf16[1024,2048]{1,0:T(8,128)(2,1)} async-done(((bf16[256,2048]{1,0:T(8,128)(2,1)}), bf16[1024,2048]{1,0:T(8,128)(2,1)}) %all-gather.14.cloned.1.call-update) | async-done | bytes 4194320 | tf_op jit(solution)/shard_map/all_gather | solution.py:105
  195.0 35.1 %while.28 = (s32[]{:T(128)}, bf16[8,256,2,128]{1,3,2,0:T(8,128)(2,1)}, f32[8,2,256]{2,1,0:T(2,128)}, bf16[8,256,128]{1,2,0:T(8,128)(2,1)}, bf16[8,256,128]{2,1,0...) while((s32[]{:T(128)}, ...), condition=%wide.region_9.10_spmd.clone, body=%wide.region_6.9_spmd.clone.sunk | while | flops 68615680 | bytes 2117469 | solution.py:155
  230.1 36.3 %all-gather.16.cloned.1.call-done = bf16[2048,1024]{1,0:T(8,128)(2,1)} async-done(((bf16[512,1024]{1,0:T(8,128)(2,1)}), bf16[2048,1024]{1,0:T(8,128)(2,1)}) %all-gather.16.cloned.1.call-update) | async-done | bytes 4194320 | tf_op jit(solution)/shard_map/all_gather | solution.py:108
  271.4 110.3 %all-gather.18.cloned.1.call-done = bf16[1024,3072]{1,0:T(8,128)(2,1)} async-done(((bf16[256,3072]{1,0:T(8,128)(2,1)}), bf16[1024,3072]{1,0:T(8,128)(2,1)}) %all-gather.18.cloned.1.call-update) | async-done | bytes 6291472 | tf_op jit(solution)/shard_map/all_gather | solution.py:159
  381.7 6.2 fusion.100
  388.0 108.8 %all-gather.20.cloned.1.call-done = bf16[1024,3072]{1,0:T(8,128)(2,1)} async-done(((bf16[256,3072]{1,0:T(8,128)(2,1)}), bf16[1024,3072]{1,0:T(8,128)(2,1)}) %all-gather.20.cloned.1.call-update) | async-done | bytes 6291472 | tf_op jit(solution)/shard_map/all_gather | solution.py:160
  496.8 6.2 fusion.101
  503.0 108.9 %all-gather.22.cloned.1.call-done = bf16[3072,1024]{1,0:T(8,128)(2,1)} async-done(((bf16[768,1024]{1,0:T(8,128)(2,1)}), bf16[3072,1024]{1,0:T(8,128)(2,1)}) %all-gather.22.cloned.1.call-update) | async-done | bytes 6291472 | tf_op jit(solution)/shard_map/all_gather | solution.py:161
  612.0 8.8 multiply_convert_fusion.1
  638.6 74.3 %while.29 = (s32[]{:T(128)}, f32[8,256,2,128]{1,3,2,0:T(8,128)}, f32[8,256,128]{2,1,0:T(8,128)}, bf16[8,256,128]{1,2,0:T(8,128)(2,1)}, bf16[8,256,128]{2,1,0:T(8...) while((s32[]{:T(128)}, f32[8,256,2,128]{1,3,2,0:T(8,128)}, ...), condition=%wide.region_14.15_spmd.clone, body=%wide.region_12.14_spmd.clone.sunk | while | flops 169442816 | bytes 5325177 | solution.py:244
  776.8 35.9 %reduce-scatter.12.cloned.1.call-done = bf16[256,1024]{1,0:T(8,128)(2,1)} async-done(((bf16[1024,1024]{1,0:T(8,128)(2,1)}), bf16[256,1024]{1,0:T(8,128)(2,1)}) %reduce-scatter.12.cloned.1.call-update) | async-done | bytes 524304 | tf_op jit(solution)/shard_map/reduce_scatter | solution.py:282
  812.7 78.3 %reduce-scatter.8.cloned.1.call-done = bf16[256,2048]{1,0:T(8,128)(2,1)} async-done(((bf16[1024,2048]{1,0:T(8,128)(2,1)}), bf16[256,2048]{1,0:T(8,128)(2,1)}) %reduce-scatter.8.cloned.1.call-update) | async-done | bytes 1048592 | tf_op jit(solution)/shard_map/reduce_scatter | solution.py:276
  890.9 79.7 %reduce-scatter.14.cloned.1.call-done = bf16[512,1024]{1,0:T(8,128)(2,1)} async-done(((bf16[2048,1024]{1,0:T(8,128)(2,1)}), bf16[512,1024]{1,0:T(8,128)(2,1)}) %reduce-scatter.14.cloned.1.call-update) | async-done | bytes 1048592 | tf_op jit(solution)/shard_map/reduce_scatter | solution.py:285
  970.6 113.4 %reduce-scatter.16.cloned.1.call-done = bf16[256,3072]{1,0:T(8,128)(2,1)} async-done(((bf16[1024,3072]{1,0:T(8,128)(2,1)}), bf16[256,3072]{1,0:T(8,128)(2,1)}) %reduce-scatter.16.cloned.1.call-update) | async-done | bytes 1572880 | tf_op jit(solution)/shard_map/reduce_scatter | solution.py:191
  1084.1 113.6 %reduce-scatter.18.cloned.1.call-done = bf16[256,3072]{1,0:T(8,128)(2,1)} async-done(((bf16[1024,3072]{1,0:T(8,128)(2,1)}), bf16[256,3072]{1,0:T(8,128)(2,1)}) %reduce-scatter.18.cloned.1.call-update) | async-done | bytes 1572880 | tf_op jit(solution)/shard_map/reduce_scatter | solution.py:194
  1197.7 113.5 %reduce-scatter.20.cloned.1.call-done = bf16[768,1024]{1,0:T(8,128)(2,1)} async-done(((bf16[3072,1024]{1,0:T(8,128)(2,1)}), bf16[768,1024]{1,0:T(8,128)(2,1)}) %reduce-scatter.20.cloned.1.call-update) | async-done | bytes 1572880 | tf_op jit(solution)/shard_map/reduce_scatter | solution.py:197
  1320.4 10.9 all-reduce.4
  1331.5 12.9 all-reduce.2
  1344.5 38.4 %psum.74 = f32[2,128]{1,0:T(2,128)S(1)} all-reduce(f32[2,128]{1,0:T(2,128)S(1)} %pad_maximum_fusion.2), channel_id=1, replica_groups=mesh['rep'=8,'fsdp'=4] {'rep','fsdp'}, use_global_device_ids=true, to_apply=%region_31.32 | all-reduce | flops 256 | bytes 2048 | tf_op jit(solution)/shard_map/psum | solution.py:264
  1390.8 48.7 %all-reduce.7.cloned.1.call-done = (bf16[256,2048]{1,0:T(8,128)(2,1)}, bf16[256,1024]{1,0:T(8,128)(2,1)}, bf16[256,1024]{1,0:T(8,128)(2,1)}, bf16[512,1024]{1,0:...) async-done(((bf16[256,2048]{1,0:T(8,128)(2,1)}, bf16[256,1024]{1,0:T(8,128)(2,1)}, bf16[256,1024]{1,0:T(8,128)(2,1)}, ...) | async-done | bytes 7864336 | tf_op jit(solution)/shard_map/psum | solution.py:293
  (337 shorter events, 252.8 us)
Async XLA Ops:
  7.2 51.1 %all-gather.12.cloned.1.call-start = ((), (), s32[]{:S(2)}) async-start(), calls=%async_computation.8 | async-start | bytes 2621440 | tf_op jit(solution)/shard_map/all_gather | solution.py:106
  7.9 96.7 %all-gather.10.cloned.1.call-start = ((), (), s32[]{:S(2)}) async-start(), calls=%async_computation.7 | async-start | bytes 2621440 | tf_op jit(solution)/shard_map/all_gather | solution.py:107
  8.7 177.0 %all-gather.14.cloned.1.call-start = ((), (), s32[]{:S(2)}) async-start(), calls=%async_computation.9 | async-start | bytes 5242880 | tf_op jit(solution)/shard_map/all_gather | solution.py:105
  9.4 257.0 %all-gather.16.cloned.1.call-start = ((), (), s32[]{:S(2)}) async-start(), calls=%async_computation.10 | async-start | bytes 5242880 | tf_op jit(solution)/shard_map/all_gather | solution.py:108
  10.0 15.5 %copy-start = (bf16[256,1024]{1,0:T(8,128)(2,1)S(1)}, bf16[256,1024]{1,0:T(8,128)(2,1)}, u32[]{:S(2)}) copy-start(bf16[256,1024]{1,0:T(8,128)(2,1)} %param.17) | copy-start | bytes 1572868
  10.0 371.7 %all-gather.18.cloned.1.call-start = ((), (), s32[]{:S(2)}) async-start(), calls=%async_computation.11 | async-start | bytes 7864320 | tf_op jit(solution)/shard_map/all_gather | solution.py:159
  10.6 15.1 %copy-start.49 = (bf16[2,128]{1,0:T(2,128)(2,1)S(1)}, bf16[2,128]{1,0:T(2,128)(2,1)}, u32[]{:S(2)}) copy-start(bf16[2,128]{1,0:T(2,128)(2,1)} %param.23) | copy-start | bytes 1540
  10.6 17.1 %copy-start.50 = (bf16[256]{0:T(256)(128)(2,1)S(1)}, bf16[256]{0:T(256)(128)(2,1)}, u32[]{:S(2)}) copy-start(bf16[256]{0:T(256)(128)(2,1)} %param.25) | copy-start | bytes 1540
  10.6 486.2 %all-gather.20.cloned.1.call-start = ((), (), s32[]{:S(2)}) async-start(), calls=%async_computation.12 | async-start | bytes 7864320 | tf_op jit(solution)/shard_map/all_gather | solution.py:160
  11.2 600.8 %all-gather.22.cloned.1.call-start = ((), (), s32[]{:S(2)}) async-start(), calls=%async_computation.13 | async-start | bytes 7864320 | tf_op jit(solution)/shard_map/all_gather | solution.py:161
  11.9 764.9 %reduce-scatter.10.cloned.1.call-start = ((), (), s32[]{:S(2)}) async-start(), calls=%async_computation.15 | async-start | bytes 2621440 | tf_op jit(solution)/shard_map/reduce_scatter | solution.py:279
  25.7 78.8 %copy-start.30 = (f32[256]{0:T(256)}, f32[256]{0:T(256)S(1)}, u32[]{:S(2)}) copy-start(f32[256]{0:T(256)S(1)} %add_rsqrt_fusion.3) | copy-start | bytes 3076
  26.3 35.0 %copy-start.42 = (f32[128]{0:T(128)}, f32[128]{0:T(128)S(1)}, u32[]{:S(2)}) copy-start(f32[128]{0:T(128)S(1)} %get-tuple-element.285) | copy-start | bytes 1540
  37.2 71.9 %copy-start.24 = (f32[256,64]{1,0:T(8,128)}, f32[256,64]{1,0:T(8,128)S(1)}, u32[]{:S(2)}) copy-start(f32[256,64]{1,0:T(8,128)S(1)} %get-tuple-element.282) | copy-start | bytes 196612
  230.1 40.2 %copy-start.11 = (bf16[8,256,128]{2,1,0:T(8,128)(2,1)}, bf16[8,256,128]{2,1,0:T(8,128)(2,1)S(1)}, u32[]{:S(2)}) copy-start(bf16[8,256,128]{2,1,0:T(8,128)(2,1)S(1)} %get-tuple-element.527) | copy-start | bytes 1572868
  620.8 6.0 copy-start.45
  724.2 88.5 %reduce-scatter.12.cloned.1.call-start = ((), (), s32[]{:S(2)}) async-start(), calls=%async_computation.16 | async-start | bytes 2621440 | tf_op jit(solution)/shard_map/reduce_scatter | solution.py:282
  727.5 163.4 %reduce-scatter.8.cloned.1.call-start = ((), (), s32[]{:S(2)}) async-start(), calls=%async_computation.14 | async-start | bytes 5242880 | tf_op jit(solution)/shard_map/reduce_scatter | solution.py:276
  752.1 218.5 %reduce-scatter.14.cloned.1.call-start = ((), (), s32[]{:S(2)}) async-start(), calls=%async_computation.17 | async-start | bytes 5242880 | tf_op jit(solution)/shard_map/reduce_scatter | solution.py:285
  757.9 326.2 %reduce-scatter.16.cloned.1.call-start = ((), (), s32[]{:S(2)}) async-start(), calls=%async_computation.18 | async-start | bytes 7864320 | tf_op jit(solution)/shard_map/reduce_scatter | solution.py:191
  763.8 433.9 %reduce-scatter.18.cloned.1.call-start = ((), (), s32[]{:S(2)}) async-start(), calls=%async_computation.19 | async-start | bytes 7864320 | tf_op jit(solution)/shard_map/reduce_scatter | solution.py:194
  769.8 541.4 %reduce-scatter.20.cloned.1.call-start = ((), (), s32[]{:S(2)}) async-start(), calls=%async_computation.20 | async-start | bytes 7864320 | tf_op jit(solution)/shard_map/reduce_scatter | solution.py:197
  776.7 662.8 %all-reduce.7.cloned.1.call-start = ((), (), s32[]{:S(2)}) async-start(), calls=%async_computation.21 | async-start | bytes 15728640 | tf_op jit(solution)/shard_map/psum | solution.py:293
  1318.3 26.1 %copy-start.37 = (f32[1024]{0:T(1024)S(1)}, f32[1024]{0:T(1024)}, u32[]{:S(2)}) copy-start(f32[1024]{0:T(1024)} %get-tuple-element.269) | copy-start | bytes 12292
  (43 other events, 111.7 us)
Sparse Core Ops, SparseCore 0:
  9.6 48.6 all-gather.11
  59.9 44.6 all-gather.9
  106.1 79.4 all-gather.13
  187.1 79.2 all-gather.15
  267.8 113.8 all-gather.17
  383.2 113.5 all-gather.19
  498.4 113.5 all-gather.21
  724.3 42.1 reduce-scatter.9
  769.5 43.1 reduce-scatter.11
  814.8 76.0 reduce-scatter.7
  893.3 77.2 reduce-scatter.13
  972.8 111.2 reduce-scatter.15
  1086.4 111.2 reduce-scatter.17
  1199.9 111.2 reduce-scatter.19
  1315.2 124.2 all-reduce.6
where the time goes:
time: 1470 us; the launch traced here: 1460 us
  waiting for transfers between devices  1090 us (74%)
  matrix products  172 us (12%)
  blocking collectives  82.7 us (6%)
  other arithmetic  54.4 us (4%)
  local copies, waits for them, and re-layouts  42.1 us (3%)
  between operations  15.4 us (1%)
    reduce_scatter x1, waiting for transfers between devices, per_device(): lax.psum_scatter(grad_up.astype(jnp.bfloat16), 'fsdp', scatter_dimension=...  114 us
    reduce_scatter x1, waiting for transfers between devices, per_device(): lax.psum_scatter(grad_down.astype(jnp.bfloat16), 'fsdp', scatter_dimensio...  113 us
    reduce_scatter x1, waiting for transfers between devices, per_device(): lax.psum_scatter(grad_gate.astype(jnp.bfloat16), 'fsdp', scatter_dimensio...  113 us
    all_gather x1, waiting for transfers between devices, per_device(): lax.all_gather(w_gate, 'fsdp', axis=0, tiled=True)  110 us
    all_gather x1, waiting for transfers between devices, per_device(): lax.all_gather(w_down, 'fsdp', axis=0, tiled=True)  109 us
    all_gather x1, waiting for transfers between devices, per_device(): lax.all_gather(w_up, 'fsdp', axis=0, tiled=True)  109 us
    reduce_scatter x1, waiting for transfers between devices, per_device(): lax.psum_scatter(grad_out.astype(jnp.bfloat16), 'fsdp', scatter_dimension...  79.7 us
    reduce_scatter x1, waiting for transfers between devices, per_device(): lax.psum_scatter(grad_query.astype(jnp.bfloat16), 'fsdp', scatter_dimensi...  78.3 us
  transfers between devices with their start and end apart: 15, of which 14 were waited for; matrix products, arithmetic and copies ran while one was open for 9% of the time, Pallas kernels for 0%

commit v1 on v0

--- a/solution.py
+++ b/solution.py
@@ -10,6 +10,27 @@
 EPS = 1e-06
 ROPE_BASE = 1000000.0
 NEG_FILL = -1e30
+
+
+def ring_gather(x, axis, dim):
+    size, position, rows = (lax.axis_size(axis), lax.axis_index(axis), x.shape[dim])
+    right = [(i, (i + 1) % size) for i in range(size)]
+    left = [(i, (i - 1) % size) for i in range(size)]
+    whole = jnp.zeros((*x.shape[:dim], size * rows, *x.shape[dim + 1 :]), x.dtype)
+    whole = lax.dynamic_update_slice_in_dim(whole, x, position * rows, axis=dim)
+    from_left = from_right = x
+    half = size // 2
+    for lap in range(1, half + 1):
+        from_left = lax.ppermute(from_left, axis, right)
+        whole = lax.dynamic_update_slice_in_dim(
+            whole, from_left, (position - lap) % size * rows, axis=dim
+        )
+        if lap < size - half:
+            from_right = lax.ppermute(from_right, axis, left)
+            whole = lax.dynamic_update_slice_in_dim(
+                whole, from_right, (position + lap) % size * rows, axis=dim
+            )
+    return whole
 
 
 def layout(lengths, count_of_rows):
@@ -105,7 +126,7 @@
         lax.all_gather(w_query, "fsdp", axis=0, tiled=True),
         lax.all_gather(key_matrix, "fsdp", axis=0, tiled=True),
         lax.all_gather(value_matrix, "fsdp", axis=0, tiled=True),
-        lax.all_gather(w_out, "fsdp", axis=0, tiled=True),
+        ring_gather(w_out, "fsdp", 0),
         lax.all_gather(attn_norm, "fsdp", axis=0, tiled=True),
     )
     inputs = tokens.astype(jnp.float32)

time: 1470 us -> 1510 us (1.027)
  blocking collectives: 82.7 us -> 146 us
  waiting for transfers between devices: 1090 us -> 1050 us
    all_gather x1, blocking collectives: 12.7 us -> 76.1 us  [per_device(): lax.all_gather(attn_norm, 'fsdp', axis=0, tiled=True)]
    all_gather x1, waiting for transfers between devices: 110 us -> 66.5 us  [per_device(): lax.all_gather(w_gate, 'fsdp', axis=0, tiled=True)]
    ppermute x0 -> x3, waiting for transfers between devices: none -> 42.3 us  [the longest x2 42.3 us: ring_gather(): from_left = lax.ppermute(from_left, axis, right)]
    all_gather x1, waiting for transfers between devices: 42.1 us -> 3.73 us  [per_device(): lax.all_gather(value_matrix, 'fsdp', axis=0, tiled=True)]
    all_gather x1, waiting for transfers between devices: 36.3 us -> 61.5 us  [per_device(): lax.all_gather(w_out, 'fsdp', axis=0, tiled=True)]
    all_gather x1, waiting for transfers between devices: 21.1 us -> 0.01 us  [per_device(): lax.all_gather(key_matrix, 'fsdp', axis=0, tiled=True)]
  transfers between devices with their start and end apart: 15 -> 18, of which waited for: 14 -> 14; matrix products, arithmetic and copies ran while one was open for 9% -> 11% of each run, Pallas kernels for 0% -> 0%
where the time goes in v1:
time: 1510 us; the launch traced here: 1500 us
  waiting for transfers between devices  1050 us (70%)
  matrix products  174 us (12%)
  blocking collectives  146 us (10%)
  other arithmetic  53.6 us (4%)
  local copies, waits for them, and re-layouts  49.6 us (3%)
  between operations  15.4 us (1%)
    reduce_scatter x1, waiting for transfers between devices, per_device(): lax.psum_scatter(grad_up.astype(jnp.bfloat16), 'fsdp', scatter_dimension=...  114 us
    reduce_scatter x1, waiting for transfers between devices, per_device(): lax.psum_scatter(grad_down.astype(jnp.bfloat16), 'fsdp', scatter_dimensio...  113 us
    reduce_scatter x1, waiting for transfers between devices, per_device(): lax.psum_scatter(grad_gate.astype(jnp.bfloat16), 'fsdp', scatter_dimensio...  113 us
    all_gather x1, waiting for transfers between devices, per_device(): lax.all_gather(w_down, 'fsdp', axis=0, tiled=True)  109 us
    all_gather x1, waiting for transfers between devices, per_device(): lax.all_gather(w_up, 'fsdp', axis=0, tiled=True)  109 us
    reduce_scatter x1, waiting for transfers between devices, per_device(): lax.psum_scatter(grad_out.astype(jnp.bfloat16), 'fsdp', scatter_dimension...  79.7 us
    reduce_scatter x1, waiting for transfers between devices, per_device(): lax.psum_scatter(grad_query.astype(jnp.bfloat16), 'fsdp', scatter_dimensi...  78.3 us
    all_gather x1, blocking collectives, per_device(): lax.all_gather(attn_norm, 'fsdp', axis=0, tiled=True)  76.1 us
  transfers between devices with their start and end apart: 18, of which 14 were waited for; matrix products, arithmetic and copies ran while one was open for 11% of the time, Pallas kernels for 0%

profile of v1, /device:TPU:0, one launch (start us, length us, event | category | flops | bytes accessed | tf_op | source)
XLA Modules:
  0.0 1501.8 jit_solution(9178255721574226169)
XLA Ops:
  23.1 76.1 %all-gather = bf16[4,1,256]{2,1,0:T(2,128)(2,1)S(1)} all-gather(bf16[1,1,256]{2,1,0:T(2,128)(2,1)S(1)} %reshape.255), channel_id=1, replica_groups=mesh['rep'=8,'fsdp'=4] {'fsdp'}, dimensions={0}, use_global_device_ids=true | all-gather | bytes 2560 | tf_op jit(solution)/shard_map/all_gather | solution.py:130
  99.2 8.0 all-gather.1
  113.9 42.3 %collective-permute-done.2 = bf16[512,1024]{1,0:T(8,128)(2,1)S(1)} collective-permute-done((bf16[512,1024]{1,0:T(8,128)(2,1)S(1)}, bf16[512,1024]{1,0:T(8,128)(2,1)S(1)}, u32[]{:S(2)}, u32[]{:S(2)}) %collective-permute-start.2) | collective-permute-done | bytes 1048608 | tf_op jit(solution)/shard_map/ppermute | solution.py:24
  170.4 75.2 %all-gather.14.cloned.1.call-done = bf16[1024,2048]{1,0:T(8,128)(2,1)} async-done(((bf16[256,2048]{1,0:T(8,128)(2,1)}), bf16[1024,2048]{1,0:T(8,128)(2,1)}) %all-gather.14.cloned.1.call-update) | async-done | bytes 4194320 | tf_op jit(solution)/shard_map/all_gather | solution.py:126
  255.0 34.3 %while.28 = (s32[]{:T(128)}, bf16[8,256,2,128]{1,3,2,0:T(8,128)(2,1)}, f32[8,2,256]{2,1,0:T(2,128)}, bf16[8,256,128]{1,2,0:T(8,128)(2,1)}, bf16[8,256,128]{2,1,0...) while((s32[]{:T(128)}, ...), condition=%wide.region_9.10_spmd.clone, body=%wide.region_6.9_spmd.clone.sunk | while | flops 68615680 | bytes 2116969 | solution.py:176
  294.5 66.5 %all-gather.16.cloned.1.call-done = bf16[1024,3072]{1,0:T(8,128)(2,1)} async-done(((bf16[256,3072]{1,0:T(8,128)(2,1)}), bf16[1024,3072]{1,0:T(8,128)(2,1)}) %all-gather.16.cloned.1.call-update) | async-done | bytes 6291472 | tf_op jit(solution)/shard_map/all_gather | solution.py:180
  361.0 6.2 fusion.100
  367.3 108.8 %all-gather.18.cloned.1.call-done = bf16[1024,3072]{1,0:T(8,128)(2,1)} async-done(((bf16[256,3072]{1,0:T(8,128)(2,1)}), bf16[1024,3072]{1,0:T(8,128)(2,1)}) %all-gather.18.cloned.1.call-update) | async-done | bytes 6291472 | tf_op jit(solution)/shard_map/all_gather | solution.py:181
  476.1 6.2 fusion.101
  482.3 108.8 %all-gather.20.cloned.1.call-done = bf16[3072,1024]{1,0:T(8,128)(2,1)} async-done(((bf16[768,1024]{1,0:T(8,128)(2,1)}), bf16[3072,1024]{1,0:T(8,128)(2,1)}) %all-gather.20.cloned.1.call-update) | async-done | bytes 6291472 | tf_op jit(solution)/shard_map/all_gather | solution.py:182
  591.1 8.8 multiply_convert_fusion.1
  610.2 61.5 %all-gather.22.cloned.1.call-done = bf16[2048,1024]{1,0:T(8,128)(2,1)} async-done(((bf16[512,1024]{1,0:T(8,128)(2,1)}), bf16[2048,1024]{1,0:T(8,128)(2,1)}) %all-gather.22.cloned.1.call-update) | async-done | bytes 4194320 | tf_op jit(solution)/shard_map/all_gather | solution.py:235
  681.7 73.5 %while.29 = (s32[]{:T(128)}, f32[8,256,2,128]{1,3,2,0:T(8,128)}, f32[8,256,128]{2,1,0:T(8,128)}, bf16[8,256,128]{1,2,0:T(8,128)(2,1)}, bf16[8,256,128]{2,1,0:T(8...) while((s32[]{:T(128)}, f32[8,256,2,128]{1,3,2,0:T(8,128)}, ...), condition=%wide.region_14.15_spmd.clone, body=%wide.region_12.14_spmd.clone.sunk | while | flops 169442816 | bytes 5325185 | solution.py:265
  819.3 36.0 %reduce-scatter.12.cloned.1.call-done = bf16[256,1024]{1,0:T(8,128)(2,1)} async-done(((bf16[1024,1024]{1,0:T(8,128)(2,1)}), bf16[256,1024]{1,0:T(8,128)(2,1)}) %reduce-scatter.12.cloned.1.call-update) | async-done | bytes 524304 | tf_op jit(solution)/shard_map/reduce_scatter | solution.py:303
  855.3 78.3 %reduce-scatter.8.cloned.1.call-done = bf16[256,2048]{1,0:T(8,128)(2,1)} async-done(((bf16[1024,2048]{1,0:T(8,128)(2,1)}), bf16[256,2048]{1,0:T(8,128)(2,1)}) %reduce-scatter.8.cloned.1.call-update) | async-done | bytes 1048592 | tf_op jit(solution)/shard_map/reduce_scatter | solution.py:297
  933.5 79.7 %reduce-scatter.14.cloned.1.call-done = bf16[512,1024]{1,0:T(8,128)(2,1)} async-done(((bf16[2048,1024]{1,0:T(8,128)(2,1)}), bf16[512,1024]{1,0:T(8,128)(2,1)}) %reduce-scatter.14.cloned.1.call-update) | async-done | bytes 1048592 | tf_op jit(solution)/shard_map/reduce_scatter | solution.py:306
  1013.2 113.4 %reduce-scatter.16.cloned.1.call-done = bf16[256,3072]{1,0:T(8,128)(2,1)} async-done(((bf16[1024,3072]{1,0:T(8,128)(2,1)}), bf16[256,3072]{1,0:T(8,128)(2,1)}) %reduce-scatter.16.cloned.1.call-update) | async-done | bytes 1572880 | tf_op jit(solution)/shard_map/reduce_scatter | solution.py:212
  1126.7 113.6 %reduce-scatter.18.cloned.1.call-done = bf16[256,3072]{1,0:T(8,128)(2,1)} async-done(((bf16[1024,3072]{1,0:T(8,128)(2,1)}), bf16[256,3072]{1,0:T(8,128)(2,1)}) %reduce-scatter.18.cloned.1.call-update) | async-done | bytes 1572880 | tf_op jit(solution)/shard_map/reduce_scatter | solution.py:215
  1240.3 113.5 %reduce-scatter.20.cloned.1.call-done = bf16[768,1024]{1,0:T(8,128)(2,1)} async-done(((bf16[3072,1024]{1,0:T(8,128)(2,1)}), bf16[768,1024]{1,0:T(8,128)(2,1)}) %reduce-scatter.20.cloned.1.call-update) | async-done | bytes 1572880 | tf_op jit(solution)/shard_map/reduce_scatter | solution.py:218
  1362.0 11.0 all-reduce.4
  1373.1 12.9 all-reduce.2
  1386.0 38.2 %psum.74 = f32[2,128]{1,0:T(2,128)S(1)} all-reduce(f32[2,128]{1,0:T(2,128)S(1)} %pad_maximum_fusion.2), channel_id=1, replica_groups=mesh['rep'=8,'fsdp'=4] {'rep','fsdp'}, use_global_device_ids=true, to_apply=%region_31.32 | all-reduce | flops 256 | bytes 2048 | tf_op jit(solution)/shard_map/psum | solution.py:285
  1426.5 6.0 fusion.65
  1432.5 49.7 %all-reduce.7.cloned.1.call-done = (bf16[256,2048]{1,0:T(8,128)(2,1)}, bf16[256,1024]{1,0:T(8,128)(2,1)}, bf16[256,1024]{1,0:T(8,128)(2,1)}, bf16[512,1024]{1,0:...) async-done(((bf16[256,2048]{1,0:T(8,128)(2,1)}, bf16[256,1024]{1,0:T(8,128)(2,1)}, bf16[256,1024]{1,0:T(8,128)(2,1)}, ...) | async-done | bytes 7864336 | tf_op jit(solution)/shard_map/psum | solution.py:314
  (346 shorter events, 265.3 us)
Async XLA Ops:
  7.2 150.1 %all-gather.12.cloned.1.call-start = ((), (), s32[]{:S(2)}) async-start(), calls=%async_computation.8 | async-start | bytes 2621440 | tf_op jit(solution)/shard_map/all_gather | solution.py:127
  7.9 157.3 %all-gather.10.cloned.1.call-start = ((), (), s32[]{:S(2)}) async-start(), calls=%async_computation.7 | async-start | bytes 2621440 | tf_op jit(solution)/shard_map/all_gather | solution.py:128
  8.7 237.0 %all-gather.14.cloned.1.call-start = ((), (), s32[]{:S(2)}) async-start(), calls=%async_computation.9 | async-start | bytes 5242880 | tf_op jit(solution)/shard_map/all_gather | solution.py:126
  9.4 351.6 %all-gather.16.cloned.1.call-start = ((), (), s32[]{:S(2)}) async-start(), calls=%async_computation.10 | async-start | bytes 7864320 | tf_op jit(solution)/shard_map/all_gather | solution.py:180
  10.0 466.1 %all-gather.18.cloned.1.call-start = ((), (), s32[]{:S(2)}) async-start(), calls=%async_computation.11 | async-start | bytes 7864320 | tf_op jit(solution)/shard_map/all_gather | solution.py:181
  10.6 580.5 %all-gather.20.cloned.1.call-start = ((), (), s32[]{:S(2)}) async-start(), calls=%async_computation.12 | async-start | bytes 7864320 | tf_op jit(solution)/shard_map/all_gather | solution.py:182
  11.1 660.6 %all-gather.22.cloned.1.call-start = ((), (), s32[]{:S(2)}) async-start(), calls=%async_computation.13 | async-start | bytes 5242880 | tf_op jit(solution)/shard_map/all_gather | solution.py:235
  11.2 96.7 %collective-permute-start = (bf16[512,1024]{1,0:T(8,128)(2,1)}, bf16[512,1024]{1,0:T(8,128)(2,1)S(1)}, u32[]{:S(2)}, u32[]{:S(2)}) collective-permute-start(bf16[512,1024]{1,0:T(8,128)(2,1)} %param.24), channel_id=1, source_target_pairs={{0,1},{1,2},{2,3},{3,0},{4,5},{5,6},{6,7},{7,4},{8,9},{9,10},{10,1... | collective-permute-start | bytes 3145736 | tf_op jit(solution)/shard_map/ppermute | solution.py:24
  14.3 98.6 %collective-permute-start.1 = (bf16[512,1024]{1,0:T(8,128)(2,1)}, bf16[512,1024]{1,0:T(8,128)(2,1)S(1)}, u32[]{:S(2)}, u32[]{:S(2)}) collective-permute-start(bf16[512,1024]{1,0:T(8,128)(2,1)} %param.24), channel_id=1, source_target_pairs={{0,3},{1,0},{2,1},{3,2},{4,7},{5,4},{6,5},{7,6},{8,11},{9,8},{10,9... | collective-permute-start | bytes 3145736 | tf_op jit(solution)/shard_map/ppermute | solution.py:29
  16.4 802.9 %reduce-scatter.10.cloned.1.call-start = ((), (), s32[]{:S(2)}) async-start(), calls=%async_computation.15 | async-start | bytes 2621440 | tf_op jit(solution)/shard_map/reduce_scatter | solution.py:300
  19.0 80.2 %copy-start.49 = (bf16[256]{0:T(256)(128)(2,1)S(1)}, bf16[256]{0:T(256)(128)(2,1)}, u32[]{:S(2)}) copy-start(bf16[256]{0:T(256)(128)(2,1)} %param.25) | copy-start | bytes 1540
  22.5 142.7 %copy-start.30 = (f32[256]{0:T(256)}, f32[256]{0:T(256)S(1)}, u32[]{:S(2)}) copy-start(f32[256]{0:T(256)S(1)} %add_rsqrt_fusion.3) | copy-start | bytes 3076
  23.1 137.2 %copy-start.42 = (f32[128]{0:T(128)}, f32[128]{0:T(128)S(1)}, u32[]{:S(2)}) copy-start(f32[128]{0:T(128)S(1)} %get-tuple-element.285) | copy-start | bytes 1540
  107.9 48.3 %collective-permute-start.2 = (bf16[512,1024]{1,0:T(8,128)(2,1)S(1)}, bf16[512,1024]{1,0:T(8,128)(2,1)S(1)}, u32[]{:S(2)}, u32[]{:S(2)}) collective-permute-start(bf16[512,1024]{1,0:T(8,128)(2,1)S(1)} %collective-permute-done), channel_id=1, source_target_pairs={{0,1},{1,2},{2,3},{3,0},{4,5},{5,6},{6,7},{7,4},{8,9},{9,10},{10,1... | collective-permute-start | bytes 3145736 | tf_op jit(solution)/shard_map/ppermute | solution.py:24
  111.8 57.9 %copy-start.25 = (f32[256,64]{1,0:T(8,128)}, f32[256,64]{1,0:T(8,128)S(1)}, u32[]{:S(2)}) copy-start(f32[256,64]{1,0:T(8,128)S(1)} %get-tuple-element.282) | copy-start | bytes 196612
  599.9 6.1 copy-start.45
  766.5 88.8 %reduce-scatter.12.cloned.1.call-start = ((), (), s32[]{:S(2)}) async-start(), calls=%async_computation.16 | async-start | bytes 2621440 | tf_op jit(solution)/shard_map/reduce_scatter | solution.py:303
  769.8 163.7 %reduce-scatter.8.cloned.1.call-start = ((), (), s32[]{:S(2)}) async-start(), calls=%async_computation.14 | async-start | bytes 5242880 | tf_op jit(solution)/shard_map/reduce_scatter | solution.py:297
  794.5 218.7 %reduce-scatter.14.cloned.1.call-start = ((), (), s32[]{:S(2)}) async-start(), calls=%async_computation.17 | async-start | bytes 5242880 | tf_op jit(solution)/shard_map/reduce_scatter | solution.py:306
  800.3 326.4 %reduce-scatter.16.cloned.1.call-start = ((), (), s32[]{:S(2)}) async-start(), calls=%async_computation.18 | async-start | bytes 7864320 | tf_op jit(solution)/shard_map/reduce_scatter | solution.py:212
  806.3 434.0 %reduce-scatter.18.cloned.1.call-start = ((), (), s32[]{:S(2)}) async-start(), calls=%async_computation.19 | async-start | bytes 7864320 | tf_op jit(solution)/shard_map/reduce_scatter | solution.py:215
  812.2 541.5 %reduce-scatter.20.cloned.1.call-start = ((), (), s32[]{:S(2)}) async-start(), calls=%async_computation.20 | async-start | bytes 7864320 | tf_op jit(solution)/shard_map/reduce_scatter | solution.py:218
  819.2 662.9 %all-reduce.7.cloned.1.call-start = ((), (), s32[]{:S(2)}) async-start(), calls=%async_computation.21 | async-start | bytes 15728640 | tf_op jit(solution)/shard_map/psum | solution.py:314
  1361.0 25.0 %copy-start.37 = (f32[1024]{0:T(1024)S(1)}, f32[1024]{0:T(1024)}, u32[]{:S(2)}) copy-start(f32[1024]{0:T(1024)} %get-tuple-element.269) | copy-start | bytes 12292
  (45 other events, 114.0 us)
Sparse Core Ops, SparseCore 0:
  9.6 81.0 all-gather.11
  92.3 72.8 all-gather.9
  166.8 78.8 all-gather.13
  247.1 113.8 all-gather.15
  362.4 113.5 all-gather.17
  477.5 113.5 all-gather.19
  592.7 78.9 all-gather.21
  766.6 42.3 reduce-scatter.9
  812.0 43.1 reduce-scatter.11
  857.4 76.0 reduce-scatter.7
  935.9 77.2 reduce-scatter.13
  1015.4 111.2 reduce-scatter.15
  1129.0 111.2 reduce-scatter.17
  1242.4 111.2 reduce-scatter.19
  1357.8 124.3 all-reduce.6
